TPU v7x, 256 devices: a whole 4x4x8 slice. The times are simulated.
256 devices in a mesh: row: 16 (over z, core), col: 16 (over y, x).
Axes of the slice: x: 4, y: 4, z: 8, core: 2. Of those that a mesh axis runs over, the one named last changes fastest.
Arguments:
- diag_block: float32 [512, 512], P('row', 'col'), may hold values from 0 to 1.7, as said below
- panel: float32 [16384, 512], P('row', 'col'), may hold values from -0.6 to 0.6
- slab: float32 [16384, 16384], P('row', 'col'), may hold values from -6 to 6
Outputs:
- chol_factor: float32 [512, 512], P('row', 'col')
- panel_factor: float32 [16384, 512], P('row', 'col')
- slab_update: float32 [16384, 16384], P('row', 'col')
Inputs may be any that keep to these rules, and one draw needn't show every extreme that they name: diag_block is symmetric positive definite, with smallest eigenvalue at least 0.3.
All inputs are finite; a program needn't handle non-finite values.
Results may differ from a plain program's by a relative error of at most 0.0003.
Values sent between devices are 32-bit elements; how exact they have to be, the bound alone decides.
A program may use at most 64 MiB of HBM per device.

v0:
```python
import jax
import jax.numpy as jnp
from jax import lax
from jax.sharding import PartitionSpec as P
from jax.experimental import pallas as pl
from jax.experimental.pallas import tpu as pltpu
F=jnp.float32
NB=512; BLK=128

def split(x):
    hi=x.astype(jnp.bfloat16)
    lo=(x-hi.astype(F)).astype(jnp.bfloat16)
    return hi,lo
def dot3(a,b,dims):
    ah,al=split(a); bh,bl=split(b)
    d=lambda x,y: lax.dot_general(x,y,(dims,((),())),preferred_element_type=F)
    return d(ah,bh)+(d(ah,bl)+d(al,bh))
NN=((1,),(0,)); NT=((1,),(1,))

def sweep(tiles):
    lane=lax.broadcasted_iota(jnp.int32,(8,BLK),1)
    sub=lax.broadcasted_iota(jnp.int32,(8,BLK),0)
    n=len(tiles); out=[]
    tiles=list(tiles)
    for p in range(n):
        R=tiles[p]
        rows=[jnp.broadcast_to(R[k:k+1,:],(8,BLK)) for k in range(8)]
        B={(k,i):jnp.broadcast_to(rows[k][:,8*p+i:8*p+i+1],(8,BLK)) for k in range(8) for i in range(k,8)}
        inm=(lane>=8*p)&(lane<8*p+8)
        E=[jnp.where(inm,jnp.where(lane==8*p+k,1.0,0.0),rows[k]) for k in range(8)]
        m={}; rcp=[]; rs=[]
        for k in range(8):
            r=lax.rsqrt(B[k,k]); rs.append(r); rc=r*r; rcp.append(rc)
            for i in range(k+1,8):
                m[i,k]=B[k,i]*rc
            for i in range(k+1,8):
                for j in range(i,8):
                    B[i,j]=B[i,j]-m[i,k]*B[k,j]
                E[i]=E[i]-m[i,k]*E[k]
        V=[None]*8
        for k in reversed(range(8)):
            v=E[k]*rcp[k]
            for i in range(k+1,8):
                v=v-m[i,k]*V[i]
            V[k]=v
        o=E[7]*rs[7]
        for k in range(7):
            o=jnp.where(sub==k,E[k]*rs[k],o)
        out.append(jnp.where(lane<=8*p+sub,o,0.0))
        for q in range(p+1,n):
            c=[jnp.broadcast_to(tiles[q][:,8*p+k:8*p+k+1],(8,BLK)) for k in range(8)]
            t=jnp.where(inm,0.0,tiles[q])
            acc=[c[k]*V[k] for k in range(8)]
            while len(acc)>1:
                acc=[acc[i]+acc[i+1] for i in range(0,len(acc),2)]
            tiles[q]=t-acc[0]
    return out

def chol_body(g):
    def step(b,_):
        off=pl.multiple_of(b*BLK,BLK)
        tiles=[g[pl.ds(pl.multiple_of(off+8*t,8),8),pl.ds(off,BLK)] for t in range(16)]
        out=sweep(tiles)
        for t in range(16):
            g[pl.ds(pl.multiple_of(off+8*t,8),8),pl.ds(off,BLK)]=out[t]
        for bb in range(4):
            @pl.when(b==bb)
            def _():
                o=bb*BLK; e=o+BLK
                X=g[o:e,o:e]
                if bb>0: g[o:e,:o]=dot3(X,g[o:e,:o],NN)
                if bb<3:
                    L=dot3(g[e:,o:e],X,NT)
                    Yl=g[o:e,:e]
                    U=dot3(X,g[o:e,e:],NN)
                    if bb>0: g[e:,:o]=g[e:,:o]-dot3(L,Yl[:,:o],NN)
                    g[e:,o:e]=-dot3(L,X,NN)
                    g[e:,e:]=g[e:,e:]-dot3(L,U,NN)
        return 0
    lax.fori_loop(0,4,step,0)
    for bb in range(3):
        g[bb*BLK:(bb+1)*BLK,(bb+1)*BLK:]=jnp.zeros((BLK,NB-(bb+1)*BLK),F)


def factor_kernel(a_ref, l_ref, x_ref):
    x_ref[...] = a_ref[...]
    chol_body(x_ref)
    rb, cb = l_ref.shape
    ro = pl.multiple_of(lax.axis_index("row") * rb, rb)
    co = pl.multiple_of(lax.axis_index("col") * cb, cb)
    block = dot3(a_ref[pl.ds(ro, rb), :], x_ref[pl.ds(co, cb), :], NT)
    gi = ro + lax.broadcasted_iota(jnp.int32, (rb, cb), 0)
    gj = co + lax.broadcasted_iota(jnp.int32, (rb, cb), 1)
    l_ref[...] = jnp.where(gi >= gj, block, 0.0)


def factor_and_inverse(a, rb, cb):
    return pl.pallas_call(
        factor_kernel,
        out_shape=(jax.ShapeDtypeStruct((rb, cb), F), jax.ShapeDtypeStruct((NB, NB), F)),
        in_specs=[pl.BlockSpec(memory_space=pltpu.VMEM)],
        out_specs=[pl.BlockSpec(memory_space=pltpu.VMEM)] * 2,
        compiler_params=pltpu.CompilerParams(vmem_limit_bytes=40 << 20),
        cost_estimate=pl.CostEstimate(flops=4 * 10**9, bytes_accessed=3 << 20, transcendentals=0),
    )(a)


def split_dot(ah, al, bh, bl, dims):
    d = lambda x, y: lax.dot_general(x, y, (dims, ((), ())), preferred_element_type=F)
    return d(ah, bh) + (d(ah, bl) + d(al, bh))


def update_kernel(x_ref, pr_ref, pc_ref, slab_ref, out_ref, po_ref, xh, xl, ch, cl, tmp):
    i = pl.program_id(0)

    @pl.when(i == 0)
    def _():
        h, l = split(x_ref[...])
        xh[...] = h
        xl[...] = l
        ph, plo = split(pc_ref[...])
        f = split_dot(ph, plo, xh[...], xl[...], NT)
        h, l = split(f)
        ch[...] = h
        cl[...] = l

    ph, plo = split(pr_ref[...])
    f = split_dot(ph, plo, xh[...], xl[...], NT)
    tmp[...] = f
    h, l = split(f)
    out_ref[...] = slab_ref[...] - split_dot(h, l, ch[...], cl[...], NT)
    c = lax.axis_index("col")
    w = po_ref.shape[1]
    per = 128 // w
    chunk = tmp[:, pl.ds(pl.multiple_of((c // per) * 128, 128), 128)]
    shift = lax.rem(128 - (c % per) * w, 128)
    po_ref[...] = pltpu.roll(chunk, shift, 1)[:, :w]


def update(x, pr, pc, slab, w, tile=256):
    m, n = slab.shape
    full = lambda s: pl.BlockSpec(s, lambda i: (0, 0), pipeline_mode=pl.Buffered(1))
    rows = lambda k: pl.BlockSpec((tile, k), lambda i: (i, 0))
    return pl.pallas_call(
        update_kernel,
        grid=(m // tile,),
        out_shape=(jax.ShapeDtypeStruct((m, n), F), jax.ShapeDtypeStruct((m, w), F)),
        in_specs=[full((NB, NB)), rows(NB), full((n, NB)), rows(n)],
        out_specs=[rows(n), rows(w)],
        scratch_shapes=[pltpu.VMEM((NB, NB), jnp.bfloat16)] * 2
        + [pltpu.VMEM((n, NB), jnp.bfloat16)] * 2
        + [pltpu.VMEM((tile, NB), F)],
        compiler_params=pltpu.CompilerParams(vmem_limit_bytes=48 << 20),
    )(x, pr, pc, slab)


def body(diag_block, panel, slab):
    nr, nc = lax.axis_size("row"), lax.axis_size("col")
    block = lax.all_gather(diag_block, "row", axis=0, tiled=True)
    block = lax.all_gather(block, "col", axis=1, tiled=True)
    pr = lax.all_gather(panel, "col", axis=1, tiled=True)
    pairs = [(r * nc + c, c * nc + r) for r in range(nr) for c in range(nc)]
    turned = lax.ppermute(panel, ("row", "col"), pairs)
    pc = lax.all_gather(turned, "row", axis=1, tiled=True)
    factor_out, inverse = factor_and_inverse(block, *diag_block.shape)
    out, panel_out = update(inverse, pr, pc, slab, panel.shape[1])
    return factor_out, panel_out, out


def solution(mesh):
    spec = P("row", "col")
    return jax.shard_map(
        body, mesh=mesh, in_specs=(spec, spec, spec), out_specs=(spec, spec, spec), check_vma=False
    )
```

profile of v0, /device:TPU:1, one launch (start us, length us, event | category | flops | bytes accessed | tf_op | source)
XLA Modules:
  0.0 198.1 jit_solution(17833019144769490688)
XLA Ops:
  7.2 0.0 all-gather.4.cloned.1.call-start
  7.2 22.3 %all_gather.12 = f32[512,32]{1,0:T(8,128)S(1)} all-gather(f32[32,32]{1,0:T(8,128)} %param.3), channel_id=1, replica_groups=mesh['row'=16,'col'=16] {'row'}, dimensions={0}, use_global_device_ids=true | all-gather | bytes 69632 | tf_op jit(solution)/shard_map/all_gather | solution.py:159
  29.5 0.7 copy.14
  30.2 0.0 all-gather.4.cloned.1.call-update
  30.2 0.0 all-gather.6.cloned.1.call-start
  30.3 0.7 all-gather.6.cloned.1.call-update
  31.0 0.0 all-gather.8.cloned.1.call-start
  31.0 3.2 %collective-permute-start = (f32[1024,32]{0,1:T(8,128)}, f32[1024,32]{0,1:T(8,128)S(1)}, u32[]{:S(2)}, u32[]{:S(2)}) collective-permute-start(f32[1024,32]{0,1:T(8,128)} %param.4), channel_id=1, source_target_pairs={{0,0},{1,16},{2,32},{3,48},{4,64},{5,80},{6,96},{7,112},{8,128},{9... | collective-permute-start | bytes 393224 | tf_op jit(solution)/shard_map/ppermute | solution.py:163
  34.2 3.3 %collective-permute-done = f32[1024,32]{0,1:T(8,128)S(1)} collective-permute-done((f32[1024,32]{0,1:T(8,128)}, f32[1024,32]{0,1:T(8,128)S(1)}, u32[]{:S(2)}, u32[]{:S(2)}) %collective-permute-start) | collective-permute-done | bytes 131104 | tf_op jit(solution)/shard_map/ppermute | solution.py:163
  37.5 0.0 copy-start.2
  37.5 0.7 copy-done.2
  38.2 0.0 all-gather.8.cloned.1.call-update
  38.2 40.8 %all-gather.4.cloned.1.call-done = f32[512,512]{0,1:T(8,128)} async-done(((f32[512,32]{0,1:T(8,128)}), f32[512,512]{0,1:T(8,128)}) %all-gather.4.cloned.1.call-update) | async-done | bytes 1048592 | tf_op jit(solution)/shard_map/all_gather | solution.py:160
  79.0 1.6 copy.15.a_ref
  80.5 25.9 %shard_map.58 = (f32[32,32]{1,0:T(8,128)}, f32[512,512]{1,0:T(8,128)S(1)}) custom-call(f32[512,512]{1,0:T(8,128)S(1)} %copy.15.a_ref), custom_call_target="tpu_custom_call" | custom-call | flops 4000000000 | bytes 3145728 | tf_op jit(solution)/shard_map/pallas_call | solution.py:98
  106.4 24.9 %all-gather.6.cloned.1.call-done = f32[1024,512]{0,1:T(8,128)} async-done(((f32[1024,32]{0,1:T(8,128)}), f32[1024,512]{0,1:T(8,128)}) %all-gather.6.cloned.1.call-update) | async-done | bytes 2097168 | tf_op jit(solution)/shard_map/all_gather | solution.py:161
  131.3 1.9 copy.16.pr_ref
  133.3 40.9 %all-gather.8.cloned.1.call-done = f32[1024,512]{0,1:T(8,128)} async-done(((f32[1024,32]{0,1:T(8,128)}), f32[1024,512]{0,1:T(8,128)}) %all-gather.8.cloned.1.call-update) | async-done | bytes 2097168 | tf_op jit(solution)/shard_map/all_gather | solution.py:164
  174.2 2.9 %copy.17.pc_ref = f32[1024,512]{1,0:T(8,128)} copy(f32[1024,512]{0,1:T(8,128)} %all-gather.8.cloned.1.call-done) | data formatting | bytes 4194304 | tf_op jit(solution)/shard_map/all_gather | solution.py:164
  177.0 0.0 copy-start
  177.0 1.6 copy-done
  178.6 10.2 %shard_map.59 = (f32[1024,1024]{1,0:T(8,128)}, f32[1024,32]{1,0:T(8,128)S(1)}) custom-call(f32[512,512]{1,0:T(8,128)S(1)} %get-tuple-element.8.x_ref, f32[1024,512]{1,0:T(8,128)S(1)} %copy.16.pr_ref, f32[1024,512]{1,0:T(8,128)S(1)} %copy-done, f32[1024,1024]{1,0:T(8,128)} %slab_ref.1), custom_call_target="tpu_custom_call" | custom-call | tf_op jit(solution)/shard_map/pallas_call | solution.py:144
  188.9 0.0 copy-start.1
  188.9 0.8 copy-done.1
  189.7 1.9 copy.18
Async XLA Ops:
  7.2 71.8 %all-gather.4.cloned.1.call-start = ((), (), s32[]{:S(2)}) async-start(), calls=%async_computation | async-start | bytes 1114112 | tf_op jit(solution)/shard_map/all_gather | solution.py:160
  30.2 101.1 %all-gather.6.cloned.1.call-start = ((), (), s32[]{:S(2)}) async-start(), calls=%async_computation.1 | async-start | bytes 2228224 | tf_op jit(solution)/shard_map/all_gather | solution.py:161
  31.0 143.2 %all-gather.8.cloned.1.call-start = ((), (), s32[]{:S(2)}) async-start(), calls=%async_computation.2 | async-start | bytes 2228224 | tf_op jit(solution)/shard_map/all_gather | solution.py:164
  31.0 6.5 %collective-permute-start = (f32[1024,32]{0,1:T(8,128)}, f32[1024,32]{0,1:T(8,128)S(1)}, u32[]{:S(2)}, u32[]{:S(2)}) collective-permute-start(f32[1024,32]{0,1:T(8,128)} %param.4), channel_id=1, source_target_pairs={{0,0},{1,16},{2,32},{3,48},{4,64},{5,80},{6,96},{7,112},{8,128},{9... | collective-permute-start | bytes 393224 | tf_op jit(solution)/shard_map/ppermute | solution.py:163
  37.5 0.7 copy-start.2
  177.0 1.6 copy-start
  188.9 0.8 copy-start.1
Sparse Core Ops, SparseCore 0:
  30.4 48.5 all-gather.3
  81.4 49.8 all-gather.5
  133.7 40.3 all-gather.7
where the time goes:
time: 198 us
  waiting for transfers between devices  111 us (56%)
  Pallas kernels  36.1 us (18%)
  blocking collectives  22.3 us (11%)
  between operations  13.8 us (7%)
  local copies, waits for them, and re-layouts  12 us (6%)
  starting transfers between devices  3.29 us (2%)
    all_gather x1, waiting for transfers between devices, body(): pc = lax.all_gather(turned, 'row', axis=1, tiled=True)  40.9 us
    all_gather x1, waiting for transfers between devices, body(): block = lax.all_gather(block, 'col', axis=1, tiled=True)  40.8 us
    pallas_call x1, Pallas kernels, factor_and_inverse(): pl.pallas_call(factor_kernel, out_shape=(jax.ShapeDtypeStruct((rb, cb), F...  25.9 us
    all_gather x1, waiting for transfers between devices, body(): pr = lax.all_gather(panel, 'col', axis=1, tiled=True)  24.9 us
    all_gather x1, blocking collectives, body(): block = lax.all_gather(diag_block, 'row', axis=0, tiled=True)  22.3 us
    pallas_call x1, Pallas kernels, update(): pl.pallas_call(update_kernel, grid=(m // tile,), out_shape=(jax.ShapeDtyp...  10.2 us
    unnamed x7, local copies, waits for them, and re-layouts  4.91 us
  transfers between devices with their start and end apart: 4, of which 4 were waited for; matrix products, arithmetic and copies ran while one was open for 2% of the time, Pallas kernels for 13%

commit v1 on v0

--- a/solution.py
+++ b/solution.py
@@ -56,7 +56,7 @@
             tiles[q]=t-acc[0]
     return out
 
-def chol_body(g):
+def chol_body(g, hook):
     def step(b,_):
         off=pl.multiple_of(b*BLK,BLK)
         tiles=[g[pl.ds(pl.multiple_of(off+8*t,8),8),pl.ds(off,BLK)] for t in range(16)]
@@ -76,33 +76,168 @@
                     if bb>0: g[e:,:o]=g[e:,:o]-dot3(L,Yl[:,:o],NN)
                     g[e:,o:e]=-dot3(L,X,NN)
                     g[e:,e:]=g[e:,e:]-dot3(L,U,NN)
+                hook(bb)
         return 0
     lax.fori_loop(0,4,step,0)
     for bb in range(3):
         g[bb*BLK:(bb+1)*BLK,(bb+1)*BLK:]=jnp.zeros((BLK,NB-(bb+1)*BLK),F)
 
 
-def factor_kernel(a_ref, l_ref, x_ref):
+MESH = pl.DeviceIdType.MESH
+
+
+def factor_kernel(
+    diag_ref, pt_ref, l_ref, x_ref, pr_ref, pc_ref, strip, a_ref,
+    s1, r1, s2, r2, s3, r3, s4, r4, s5, r5, s6, r6, own,
+):
+    r = lax.axis_index("row")
+    c = lax.axis_index("col")
+    n = 16
+    w = pt_ref.shape[0]
+    core = lax.rem(r, 2)
+    other = r + 1 - 2 * core
+    at = lambda i: pl.ds(pl.multiple_of(i * w, w), w)
+
+    barrier = pltpu.get_barrier_semaphore()
+
+    def greet(t, _):
+        pl.semaphore_signal(barrier, 1, device_id=(lax.rem(r + t, n), c), device_id_type=MESH)
+        pl.semaphore_signal(barrier, 1, device_id=(r, lax.rem(c + t, n)), device_id_type=MESH)
+        return 0
+
+    lax.fori_loop(1, n, greet, 0)
+
+    @pl.when(r != c)
+    def _():
+        pl.semaphore_signal(barrier, 1, device_id=(c, r), device_id_type=MESH)
+
+    pl.semaphore_wait(barrier, 2 * (n - 1) + jnp.where(r == c, 0, 1))
+
+    def diag_copy(src, peer):
+        return pltpu.make_async_remote_copy(
+            diag_ref, strip.at[at(src), :], s1.at[peer], r1.at[src], device_id=(peer, c), device_id_type=MESH)
+
+    def strip_copy(src, peer):
+        return pltpu.make_async_remote_copy(
+            a_ref.at[at(src), :], a_ref.at[at(src), :], s2.at[peer], r2.at[src], device_id=(r, peer), device_id_type=MESH)
+
+    def panel_copy(src, peer):
+        return pltpu.make_async_remote_copy(
+            pt_ref, pr_ref.at[at(src), :], s3.at[peer], r3.at[src], device_id=(r, peer), device_id_type=MESH)
+
+    def turn_copy(src):
+        return pltpu.make_async_remote_copy(
+            pt_ref, pc_ref.at[at(src), :], s4, r4, device_id=(c, r), device_id_type=MESH)
+
+    def z_copy(src, peer):
+        row = 2 * src + core
+        return pltpu.make_async_remote_copy(
+            pc_ref.at[at(row), :], pc_ref.at[at(row), :], s5.at[peer], r5.at[src],
+            device_id=(2 * peer + core, c), device_id_type=MESH)
+
+    def twin_copy(z, side):
+        row = 2 * z + side
+        return pltpu.make_async_remote_copy(
+            pc_ref.at[at(row), :], pc_ref.at[at(row), :], s6.at[z], r6.at[z],
+            device_id=(other, c), device_id_type=MESH)
+
+    def each(count, me, fn):
+        def step(t, _):
+            fn(lax.rem(me + t, count))
+            return 0
+        lax.fori_loop(1, count, step, 0)
+
+    each(n, r, lambda p: diag_copy(r, p).start())
+
+    @pl.when(r != c)
+    def _():
+        turn_copy(c).start()
+
+    @pl.when(r == c)
+    def _():
+        cp = pltpu.make_async_copy(pt_ref, pc_ref.at[at(r), :], r4)
+        cp.start()
+
+    mine = pltpu.make_async_copy(pt_ref, pr_ref.at[at(c), :], own)
+    mine.start()
+    strip[at(r), :] = diag_ref[...]
+    each(n, r, lambda p: diag_copy(p, p).wait_recv())
+    a_ref[at(c), :] = strip[...].T
+    each(n, c, lambda p: strip_copy(c, p).start())
+    each(n, c, lambda p: panel_copy(c, p).start())
+
+    z = r // 2
+
+    @pl.when(r != c)
+    def _():
+        turn_copy(r).wait_recv()
+
+    @pl.when(r == c)
+    def _():
+        pltpu.make_async_copy(pt_ref, pc_ref.at[at(r), :], r4).wait()
+
+    each(n // 2, z, lambda p: z_copy(z, p).start())
+    each(n, c, lambda p: strip_copy(p, p).wait_recv())
     x_ref[...] = a_ref[...]
-    chol_body(x_ref)
+
+    def hook(b):
+        if b == 2:
+            twin_copy(z, core).start()
+
+            def forward(p):
+                z_copy(p, p).wait_recv()
+                twin_copy(p, core).start()
+
+            each(n // 2, z, forward)
+
+    chol_body(x_ref, hook)
+
     rb, cb = l_ref.shape
-    ro = pl.multiple_of(lax.axis_index("row") * rb, rb)
-    co = pl.multiple_of(lax.axis_index("col") * cb, cb)
-    block = dot3(a_ref[pl.ds(ro, rb), :], x_ref[pl.ds(co, cb), :], NT)
-    gi = ro + lax.broadcasted_iota(jnp.int32, (rb, cb), 0)
-    gj = co + lax.broadcasted_iota(jnp.int32, (rb, cb), 1)
+    block = dot3(a_ref[at(r), :], x_ref[at(c), :], NT)
+    gi = r * rb + lax.broadcasted_iota(jnp.int32, (rb, cb), 0)
+    gj = c * cb + lax.broadcasted_iota(jnp.int32, (rb, cb), 1)
     l_ref[...] = jnp.where(gi >= gj, block, 0.0)
 
-
-def factor_and_inverse(a, rb, cb):
+    each(n, r, lambda p: diag_copy(r, p).wait_send())
+    each(n, c, lambda p: strip_copy(c, p).wait_send())
+    each(n, c, lambda p: panel_copy(c, p).wait_send())
+    each(n, c, lambda p: panel_copy(p, p).wait_recv())
+    mine.wait()
+
+    @pl.when(r != c)
+    def _():
+        turn_copy(c).wait_send()
+
+    each(n // 2, z, lambda p: z_copy(z, p).wait_send())
+
+    def last(t, _):
+        twin_copy(t, core).wait_send()
+        twin_copy(t, 1 - core).wait_recv()
+        return 0
+
+    lax.fori_loop(0, n // 2, last, 0)
+
+
+def factor_and_gather(diag, pt):
+    w, m = pt.shape
+    dma = pltpu.SemaphoreType.DMA
+    any_space = pl.BlockSpec(memory_space=pl.ANY)
+    vmem = pl.BlockSpec(memory_space=pltpu.VMEM)
     return pl.pallas_call(
         factor_kernel,
-        out_shape=(jax.ShapeDtypeStruct((rb, cb), F), jax.ShapeDtypeStruct((NB, NB), F)),
-        in_specs=[pl.BlockSpec(memory_space=pltpu.VMEM)],
-        out_specs=[pl.BlockSpec(memory_space=pltpu.VMEM)] * 2,
-        compiler_params=pltpu.CompilerParams(vmem_limit_bytes=40 << 20),
-        cost_estimate=pl.CostEstimate(flops=4 * 10**9, bytes_accessed=3 << 20, transcendentals=0),
-    )(a)
+        out_shape=(
+            jax.ShapeDtypeStruct(diag.shape, F),
+            jax.ShapeDtypeStruct((NB, NB), F),
+            jax.ShapeDtypeStruct((NB, m), F),
+            jax.ShapeDtypeStruct((NB, m), F),
+        ),
+        in_specs=[vmem, any_space],
+        out_specs=[vmem, vmem, any_space, any_space],
+        scratch_shapes=[pltpu.VMEM((NB, w), F), pltpu.VMEM((NB, NB), F)]
+        + [dma((16,))] * 6 + [dma(()), dma(())] + [dma((8,))] * 4 + [dma(())],
+        compiler_params=pltpu.CompilerParams(
+            vmem_limit_bytes=40 << 20, collective_id=0, has_side_effects=True),
+    )(diag, pt)
 
 
 def split_dot(ah, al, bh, bl, dims):
@@ -119,52 +254,42 @@
         xh[...] = h
         xl[...] = l
         ph, plo = split(pc_ref[...])
-        f = split_dot(ph, plo, xh[...], xl[...], NT)
+        f = split_dot(xh[...], xl[...], ph, plo, NN)
         h, l = split(f)
         ch[...] = h
         cl[...] = l
 
     ph, plo = split(pr_ref[...])
-    f = split_dot(ph, plo, xh[...], xl[...], NT)
+    f = split_dot(xh[...], xl[...], ph, plo, NN)
     tmp[...] = f
-    h, l = split(f)
-    out_ref[...] = slab_ref[...] - split_dot(h, l, ch[...], cl[...], NT)
-    c = lax.axis_index("col")
-    w = po_ref.shape[1]
-    per = 128 // w
-    chunk = tmp[:, pl.ds(pl.multiple_of((c // per) * 128, 128), 128)]
-    shift = lax.rem(128 - (c % per) * w, 128)
-    po_ref[...] = pltpu.roll(chunk, shift, 1)[:, :w]
+    h, l = split(f.T)
+    out_ref[...] = slab_ref[...] - split_dot(h, l, ch[...], cl[...], NN)
+    w = po_ref.shape[0]
+    po_ref[...] = tmp[pl.ds(pl.multiple_of(lax.axis_index("col") * w, w), w), :]
 
 
 def update(x, pr, pc, slab, w, tile=256):
     m, n = slab.shape
     full = lambda s: pl.BlockSpec(s, lambda i: (0, 0), pipeline_mode=pl.Buffered(1))
     rows = lambda k: pl.BlockSpec((tile, k), lambda i: (i, 0))
+    cols = lambda k: pl.BlockSpec((k, tile), lambda i: (0, i))
     return pl.pallas_call(
         update_kernel,
         grid=(m // tile,),
-        out_shape=(jax.ShapeDtypeStruct((m, n), F), jax.ShapeDtypeStruct((m, w), F)),
-        in_specs=[full((NB, NB)), rows(NB), full((n, NB)), rows(n)],
-        out_specs=[rows(n), rows(w)],
+        out_shape=(jax.ShapeDtypeStruct((m, n), F), jax.ShapeDtypeStruct((w, m), F)),
+        in_specs=[full((NB, NB)), cols(NB), full((NB, n)), rows(n)],
+        out_specs=[rows(n), cols(w)],
         scratch_shapes=[pltpu.VMEM((NB, NB), jnp.bfloat16)] * 2
-        + [pltpu.VMEM((n, NB), jnp.bfloat16)] * 2
-        + [pltpu.VMEM((tile, NB), F)],
+        + [pltpu.VMEM((NB, n), jnp.bfloat16)] * 2
+        + [pltpu.VMEM((NB, tile), F)],
         compiler_params=pltpu.CompilerParams(vmem_limit_bytes=48 << 20),
     )(x, pr, pc, slab)
 
 
 def body(diag_block, panel, slab):
-    nr, nc = lax.axis_size("row"), lax.axis_size("col")
-    block = lax.all_gather(diag_block, "row", axis=0, tiled=True)
-    block = lax.all_gather(block, "col", axis=1, tiled=True)
-    pr = lax.all_gather(panel, "col", axis=1, tiled=True)
-    pairs = [(r * nc + c, c * nc + r) for r in range(nr) for c in range(nc)]
-    turned = lax.ppermute(panel, ("row", "col"), pairs)
-    pc = lax.all_gather(turned, "row", axis=1, tiled=True)
-    factor_out, inverse = factor_and_inverse(block, *diag_block.shape)
+    factor_out, inverse, pr, pc = factor_and_gather(diag_block, panel.T)
     out, panel_out = update(inverse, pr, pc, slab, panel.shape[1])
-    return factor_out, panel_out, out
+    return factor_out, panel_out.T, out
 
 
 def solution(mesh):

time: 198 us -> 100 us (0.51)
  the two profiles are of different devices: /device:TPU:1 before, /device:TPU:49 now
where the time goes in v1:
time: 100 us; the launch traced here: 99.9 us
  Pallas kernels  97 us (97%)
  local copies, waits for them, and re-layouts  2.22 us (2%)
    pallas_call x1, Pallas kernels, factor_and_gather(): pl.pallas_call(factor_kernel, out_shape=(jax.ShapeDtypeStruct(diag.shape,...  83.5 us
    pallas_call x1, Pallas kernels, update(): pl.pallas_call(update_kernel, grid=(m // tile,), out_shape=(jax.ShapeDtyp...  13.5 us
    unnamed x5, local copies, waits for them, and re-layouts  2.22 us

profile of v1, /device:TPU:49, one launch (start us, length us, event | category | flops | bytes accessed | tf_op | source)
XLA Modules:
  0.0 99.9 jit_solution(3540084054678194061)
XLA Ops:
  0.6 0.0 copy-start
  0.6 0.9 copy-done
  1.5 0.0 copy-start.1
  1.5 0.7 copy-done.1
  2.3 83.5 %shard_map.58 = (f32[32,32]{1,0:T(8,128)S(1)}, f32[512,512]{1,0:T(8,128)S(1)}, f32[512,1024]{1,0:T(8,128)S(1)}, f32[512,1024]{1,0:T(8,128)S(1)}) custom-call(f32[32,32]{1,0:T(8,128)S(1)} %copy-done.1, f32[32,1024]{1,0:T(8,128)S(1)} %bitcast.2), custom_call_target="tpu_custom_call" | custom-call | tf_op jit(solution)/shard_map/pallas_call | solution.py:226
  85.8 13.5 %shard_map.59 = (f32[1024,1024]{1,0:T(8,128)}, f32[32,1024]{1,0:T(8,128)}) custom-call(f32[512,512]{1,0:T(8,128)S(1)} %get-tuple-element.10.x_ref, f32[512,1024]{1,0:T(8,128)S(1)} %get-tuple-element.11.pr_ref, f32[512,1024]{1,0:T(8,128)S(1)} %get-tuple-element.12.pc_ref, f32[1024,1024]{1,0:T(8,128)} %slab_ref.1), custom_call_target="tpu_custom_call" | custom-call | tf_op jit(solution)/shard_map/pallas_call | solution.py:276
  99.3 0.6 copy.7
Async XLA Ops:
  0.6 0.9 copy-start
  1.5 0.7 copy-start.1

commit v2 on v1

v2 whole, which is shorter than its diff:
```python
import jax
import jax.numpy as jnp
from jax import lax
from jax.sharding import PartitionSpec as P
from jax.experimental import pallas as pl
from jax.experimental.pallas import tpu as pltpu
F=jnp.float32
NB=512; BLK=128

def split(x):
    hi=x.astype(jnp.bfloat16)
    lo=(x-hi.astype(F)).astype(jnp.bfloat16)
    return hi,lo
def dot3(a,b,dims):
    ah,al=split(a); bh,bl=split(b)
    d=lambda x,y: lax.dot_general(x,y,(dims,((),())),preferred_element_type=F)
    return d(ah,bh)+(d(ah,bl)+d(al,bh))
NN=((1,),(0,)); NT=((1,),(1,))

def sweep(tiles):
    lane=lax.broadcasted_iota(jnp.int32,(8,BLK),1)
    sub=lax.broadcasted_iota(jnp.int32,(8,BLK),0)
    n=len(tiles); out=[]
    tiles=list(tiles)
    for p in range(n):
        R=tiles[p]
        rows=[jnp.broadcast_to(R[k:k+1,:],(8,BLK)) for k in range(8)]
        B={(k,i):jnp.broadcast_to(rows[k][:,8*p+i:8*p+i+1],(8,BLK)) for k in range(8) for i in range(k,8)}
        inm=(lane>=8*p)&(lane<8*p+8)
        E=[jnp.where(inm,jnp.where(lane==8*p+k,1.0,0.0),rows[k]) for k in range(8)]
        m={}; rcp=[]; rs=[]
        for k in range(8):
            r=lax.rsqrt(B[k,k]); rs.append(r); rc=r*r; rcp.append(rc)
            for i in range(k+1,8):
                m[i,k]=B[k,i]*rc
            for i in range(k+1,8):
                for j in range(i,8):
                    B[i,j]=B[i,j]-m[i,k]*B[k,j]
                E[i]=E[i]-m[i,k]*E[k]
        V=[None]*8
        for k in reversed(range(8)):
            v=E[k]*rcp[k]
            for i in range(k+1,8):
                v=v-m[i,k]*V[i]
            V[k]=v
        o=E[7]*rs[7]
        for k in range(7):
            o=jnp.where(sub==k,E[k]*rs[k],o)
        out.append(jnp.where(lane<=8*p+sub,o,0.0))
        for q in range(p+1,n):
            c=[jnp.broadcast_to(tiles[q][:,8*p+k:8*p+k+1],(8,BLK)) for k in range(8)]
            t=jnp.where(inm,0.0,tiles[q])
            acc=[c[k]*V[k] for k in range(8)]
            while len(acc)>1:
                acc=[acc[i]+acc[i+1] for i in range(0,len(acc),2)]
            tiles[q]=t-acc[0]
    return out


MESH = pl.DeviceIdType.MESH


def factor_blocks(a, u, x, s, arrive, hook):
    def step(b, _):
        for bb in range(4):
            o, e = bb * BLK, (bb + 1) * BLK

            @pl.when(b == bb)
            def _():
                arrive(bb)
                if bb == 0:
                    s[...] = a[0:BLK, :]
                else:
                    wt = u[0:o, o:e].T
                    s[:, :o] = -dot3(wt, x[0:o, 0:o], NN)
                    s[:, o:] = a[o:e, o:] - dot3(wt, u[0:o, o:], NN)

        off = pl.multiple_of(b * BLK, BLK)
        out = sweep([s[8 * t : 8 * t + 8, pl.ds(off, BLK)] for t in range(16)])
        for t in range(16):
            x[pl.ds(pl.multiple_of(off + 8 * t, 8), 8), pl.ds(off, BLK)] = out[t]
        for bb in range(4):
            o, e = bb * BLK, (bb + 1) * BLK

            @pl.when(b == bb)
            def _():
                inv = x[o:e, o:e]
                u[o:e, o:] = dot3(inv, s[:, o:], NN)
                if bb > 0:
                    x[o:e, :o] = dot3(inv, s[:, :o], NN)
                if bb < 3:
                    x[o:e, e:] = jnp.zeros((BLK, NB - e), F)
                hook(bb)

        return 0

    lax.fori_loop(0, 4, step, 0)


def factor_kernel(
    diag_ref, pt_ref, l_ref, x_ref, pr_ref, pc_ref, pack, strip, tb, a_ref, u_ref, s_ref,
    s1, r1, s2, r2, sx, rx, sy, ry, sx2, rx2, sy2, ry2, st, s5, r5, s6, r6, own,
):
    r = lax.axis_index("row")
    c = lax.axis_index("col")
    n = 16
    w, m = pt_ref.shape
    z = r // 2
    core = lax.rem(r, 2)
    away = lax.rem(r - c + n, n)
    other = r + 1 - 2 * core
    cy, cx = c // 4, lax.rem(c, 4)
    at = lambda i: pl.ds(pl.multiple_of(i * w, w), w)
    at4 = lambda i: pl.ds(pl.multiple_of(i * 4 * w, 4 * w), 4 * w)
    left, right = pl.ds(0, m // 2), pl.ds(m // 2, m // 2)

    def loop(start, stop, fn):
        def step(t, _):
            fn(t)
            return 0

        lax.fori_loop(start, stop, step, 0)

    def each(count, me, fn):
        loop(1, count, lambda t: fn(lax.rem(me + t, count)))

    barrier = pltpu.get_barrier_semaphore()

    def greet(row, col):
        pl.semaphore_signal(barrier, 1, device_id=(row, col), device_id_type=MESH)

    each(n, r, lambda p: greet(p, c))
    each(n, c, lambda p: greet(r, p))
    pl.semaphore_wait(barrier, 2 * (n - 1))

    def remote(src, dst, send, recv, row, col):
        return pltpu.make_async_remote_copy(src, dst, send, recv, device_id=(row, col), device_id_type=MESH)

    pw = pack.shape[0] // n
    at8 = lambda i: pl.ds(pl.multiple_of(i * pw, pw), pw)

    def diag_copy(src, peer):
        part = pack.at[at8(src), :]
        return remote(part, part, s1.at[peer], r1.at[src], peer, c)

    def strip_copy(src, peer, q):
        part = a_ref.at[at(src), q * BLK :]
        return remote(part, part, s2.at[peer], r2.at[src], r, peer)

    def x_first(src, peer):
        return remote(pt_ref.at[:, left], pr_ref.at[at(4 * cy + src), left], sx.at[peer], rx.at[src], r, 4 * cy + peer)

    def y_first(src, peer):
        return remote(pt_ref.at[:, right], pr_ref.at[at(4 * src + cx), right], sy.at[peer], ry.at[src], r, 4 * peer + cx)

    def y_second(src, peer):
        part = pr_ref.at[at4(src), left]
        return remote(part, part, sy2.at[peer], ry2.at[src], r, 4 * peer + cx)

    def x_second(src, peer, j):
        part = pr_ref.at[at(4 * j + src), right]
        return remote(part, part, sx2.at[4 * peer + j], rx2.at[4 * src + j], r, 4 * cy + peer)

    def turn_z():
        return remote(pt_ref, tb, st.at[0], st.at[1], lax.rem(r + c, n), c)

    def turn_plane():
        return remote(tb, pc_ref.at[at(c), :], st.at[2], st.at[3], r, away)

    def turn_plane_in():
        return remote(tb, pc_ref.at[at(away), :], st.at[2], st.at[3], r, away)

    def turn_local(src, dst):
        return pltpu.make_async_copy(src, dst, own.at[1])

    def z_row(t):
        return 2 * lax.rem(z + t + 8, 8) + core

    def piece(t, side):
        return pc_ref.at[at(lax.rem(2 * lax.rem(z + t + 8, 8) + side - c + n, n)), :]

    def z_copy(i, src, to):
        part = piece(src, core)
        return remote(part, part, s5.at[i], r5.at[(src - to) % 8], z_row(to), c)

    def z_in(src):
        part = piece(src, core)
        return remote(part, part, s5.at[0], r5.at[src % 8], r, c)

    def twin_copy(t, side):
        part = piece(t, side)
        return remote(part, part, s6.at[t % 8], r6.at[t % 8], other, c)

    first = ((0, 2), (0, -2), (0, 1), (0, -1))
    relay = ((-2, 2), (-2, 1), (2, -1))

    block = diag_ref[...]
    pack[at8(r), :] = jnp.concatenate([block[pw * j : pw * j + pw, :] for j in range(w // pw)], axis=1)
    each(n, r, lambda p: diag_copy(r, p).start())
    keep = pltpu.make_async_copy(pt_ref, pr_ref.at[at(c), :], own.at[0])
    keep.start()
    each(4, cx, lambda p: x_first(cx, p).start())
    each(4, cy, lambda p: y_first(cy, p).start())

    @pl.when(c != 0)
    def _():
        turn_z().start()

    @pl.when(c == 0)
    def _():
        turn_local(pt_ref, tb).start()

    each(n, r, lambda p: diag_copy(p, p).wait_recv())
    for i in range(n):
        packed = pack[pw * i : pw * i + pw, :]
        for j in range(w // pw):
            moved = packed if j == 0 else pltpu.roll(packed, BLK - w * j, 1)
            strip[w * i + pw * j : w * i + pw * j + pw, :] = moved[:, :w]
    a_ref[at(c), :] = strip[...].T
    group = c // 4

    def strips(fn):
        for q in range(4):

            @pl.when(group == q)
            def _():
                each(n, c, lambda p: fn(p, q))

    strips(lambda p, q: strip_copy(c, p, q).start())

    @pl.when(c != 0)
    def _():
        turn_z().wait()

    @pl.when(c == 0)
    def _():
        turn_local(pt_ref, tb).wait()

    @pl.when(away != c)
    def _():
        turn_plane().start()

    @pl.when(away == c)
    def _():
        turn_local(tb, pc_ref.at[at(c), :]).start()

    def arrive(bb):
        def one(t):
            @pl.when(t != c)
            def _():
                strip_copy(t, t, bb).wait_recv()

        loop(4 * bb, 4 * bb + 4, one)
        if bb == 0:

            @pl.when(away != c)
            def _():
                turn_plane_in().wait()

            @pl.when(away == c)
            def _():
                turn_local(tb, pc_ref.at[at(c), :]).wait()

            for i, (src, to) in enumerate(first):
                z_copy(i, src, to).start()
            keep.wait()
            each(4, cx, lambda p: x_first(p, p).wait_recv())
            each(4, cy, lambda p: y_second(cy, p).start())
            each(4, cy, lambda p: y_first(p, p).wait_recv())
            for j in range(4):
                each(4, cx, lambda p: x_second(cx, p, j).start())

    def hook(bb):
        if bb == 0:
            z_in(-2).wait_recv()
            z_in(2).wait_recv()
            for i, (src, to) in enumerate(relay):
                z_copy(4 + i, src, to).start()
            for t in (0, 2, -2):
                twin_copy(t, core).start()
        if bb == 2:
            for t in (1, -1, 3, -3, 4):
                z_in(t).wait_recv()
                twin_copy(t, core).start()

    factor_blocks(a_ref, u_ref, x_ref, s_ref, arrive, hook)

    rows, cols = l_ref.shape
    per = BLK // w
    chunk = u_ref[at(c), pl.ds(pl.multiple_of((r // per) * BLK, BLK), BLK)]
    turned = pltpu.roll(chunk, lax.rem(BLK - lax.rem(r, per) * w, BLK), 1)[:, :w].T
    gi = r * w + lax.broadcasted_iota(jnp.int32, (rows, cols), 0)
    gj = c * w + lax.broadcasted_iota(jnp.int32, (rows, cols), 1)
    l_ref[...] = jnp.where(gi >= gj, turned, 0.0)

    each(n, r, lambda p: diag_copy(r, p).wait_send())
    strips(lambda p, q: strip_copy(c, p, q).wait_send())
    each(4, cx, lambda p: x_first(cx, p).wait_send())
    each(4, cy, lambda p: y_first(cy, p).wait_send())
    for i, (src, to) in enumerate(first + relay):
        z_copy(i, src, to).wait_send()
    each(4, cy, lambda p: y_second(cy, p).wait_send())
    each(4, cy, lambda p: y_second(p, p).wait_recv())
    for j in range(4):
        each(4, cx, lambda p: x_second(cx, p, j).wait_send())
        each(4, cx, lambda p: x_second(p, p, j).wait_recv())

    for t in range(8):
        twin_copy(t, core).wait_send()
        twin_copy(t, 1 - core).wait_recv()


def factor_and_gather(diag, pt):
    w, m = pt.shape
    dma = pltpu.SemaphoreType.DMA
    any_space = pl.BlockSpec(memory_space=pl.ANY)
    vmem = pl.BlockSpec(memory_space=pltpu.VMEM)
    return pl.pallas_call(
        factor_kernel,
        out_shape=(
            jax.ShapeDtypeStruct(diag.shape, F),
            jax.ShapeDtypeStruct((NB, NB), F),
            jax.ShapeDtypeStruct((NB, m), F),
            jax.ShapeDtypeStruct((NB, m), F),
        ),
        in_specs=[vmem, any_space],
        out_specs=[vmem, vmem, any_space, any_space],
        scratch_shapes=[
            pltpu.VMEM((w * NB // BLK, BLK), F),
            pltpu.VMEM((NB, w), F),
            pltpu.VMEM((w, m), F),
            pltpu.VMEM((NB, NB), F),
            pltpu.VMEM((NB, NB), F),
            pltpu.VMEM((BLK, NB), F),
        ]
        + [dma((16,))] * 4
        + [dma((4,))] * 4
        + [dma((16,)), dma((16,)), dma((4,)), dma((4,))]
        + [dma((4,)), dma((8,)), dma((8,)), dma((8,)), dma((8,)), dma((2,))],
        compiler_params=pltpu.CompilerParams(
            vmem_limit_bytes=40 << 20, collective_id=0, has_side_effects=True
        ),
    )(diag, pt)


def split_dot(ah, al, bh, bl, dims):
    d = lambda x, y: lax.dot_general(x, y, (dims, ((), ())), preferred_element_type=F)
    return d(ah, bh) + (d(ah, bl) + d(al, bh))


def update_kernel(x_ref, pr_ref, pc_ref, slab_ref, out_ref, po_ref, xh, xl, ch, cl, tmp):
    i = pl.program_id(0)

    @pl.when(i == 0)
    def _():
        h, l = split(x_ref[...])
        xh[...] = h
        xl[...] = l
        ph, plo = split(pc_ref[...])
        f = split_dot(xh[...], xl[...], ph, plo, NN)
        h, l = split(f)
        ch[...] = h
        cl[...] = l

    ph, plo = split(pr_ref[...])
    f = split_dot(xh[...], xl[...], ph, plo, NN)
    tmp[...] = f
    h, l = split(f.T)
    out_ref[...] = slab_ref[...] - split_dot(h, l, ch[...], cl[...], NN)
    w = po_ref.shape[0]
    po_ref[...] = tmp[pl.ds(pl.multiple_of(lax.axis_index("col") * w, w), w), :]


def update(x, pr, pc, slab, w, tile=256):
    m, n = slab.shape
    full = lambda s: pl.BlockSpec(s, lambda i: (0, 0), pipeline_mode=pl.Buffered(1))
    rows = lambda k: pl.BlockSpec((tile, k), lambda i: (i, 0))
    cols = lambda k: pl.BlockSpec((k, tile), lambda i: (0, i))
    return pl.pallas_call(
        update_kernel,
        grid=(m // tile,),
        out_shape=(jax.ShapeDtypeStruct((m, n), F), jax.ShapeDtypeStruct((w, m), F)),
        in_specs=[full((NB, NB)), cols(NB), full((NB, n)), rows(n)],
        out_specs=[rows(n), cols(w)],
        scratch_shapes=[pltpu.VMEM((NB, NB), jnp.bfloat16)] * 2
        + [pltpu.VMEM((NB, n), jnp.bfloat16)] * 2
        + [pltpu.VMEM((NB, tile), F)],
        compiler_params=pltpu.CompilerParams(vmem_limit_bytes=48 << 20),
    )(x, pr, pc, slab)


def body(diag_block, panel, slab):
    factor_out, inverse, pr, pc = factor_and_gather(diag_block, panel.T)
    out, panel_out = update(inverse, pr, pc, slab, panel.shape[1])
    return factor_out, panel_out.T, out


def solution(mesh):
    spec = P("row", "col")
    return jax.shard_map(
        body, mesh=mesh, in_specs=(spec, spec, spec), out_specs=(spec, spec, spec), check_vma=False
    )
```

time: 100 us -> 79.1 us (0.79)
  the two profiles are of different devices: /device:TPU:49 before, /device:TPU:33 now
where the time goes in v2:
time: 79.1 us; the launch traced here: 79 us
  Pallas kernels  76.1 us (96%)
  local copies, waits for them, and re-layouts  2.22 us (3%)
    pallas_call x1, Pallas kernels, factor_and_gather(): pl.pallas_call(factor_kernel, out_shape=(jax.ShapeDtypeStruct(diag.shape,...  62.6 us
    pallas_call x1, Pallas kernels, update(): pl.pallas_call(update_kernel, grid=(m // tile,), out_shape=(jax.ShapeDtyp...  13.5 us
    unnamed x5, local copies, waits for them, and re-layouts  2.22 us

profile of v2, /device:TPU:33, one launch (start us, length us, event | category | flops | bytes accessed | tf_op | source)
XLA Modules:
  0.0 79.0 jit_solution(7792048390812273152)
XLA Ops:
  0.6 0.0 copy-start
  0.6 0.9 %copy-done = f32[1024,32]{0,1:T(8,128)S(1)} copy-done((f32[1024,32]{0,1:T(8,128)S(1)}, f32[1024,32]{0,1:T(8,128)}, u32[]{:S(2)}) %copy-start) | copy-done | bytes 131096
  1.5 0.0 copy-start.1
  1.5 0.7 copy-done.1
  2.3 62.6 %shard_map.58 = (f32[32,32]{1,0:T(8,128)S(1)}, f32[512,512]{1,0:T(8,128)S(1)}, f32[512,1024]{1,0:T(8,128)S(1)}, f32[512,1024]{1,0:T(8,128)S(1)}) custom-call(f32[32,32]{1,0:T(8,128)S(1)} %copy-done.1, f32[32,1024]{1,0:T(8,128)S(1)} %bitcast.2), custom_call_target="tpu_custom_call" | custom-call | tf_op jit(solution)/shard_map/pallas_call | solution.py:318
  64.9 13.5 %shard_map.59 = (f32[1024,1024]{1,0:T(8,128)}, f32[32,1024]{1,0:T(8,128)}) custom-call(f32[512,512]{1,0:T(8,128)S(1)} %get-tuple-element.10.x_ref, f32[512,1024]{1,0:T(8,128)S(1)} %get-tuple-element.11.pr_ref, f32[512,1024]{1,0:T(8,128)S(1)} %get-tuple-element.12.pc_ref, f32[1024,1024]{1,0:T(8,128)} %slab_ref.1), custom_call_target="tpu_custom_call" | custom-call | tf_op jit(solution)/shard_map/pallas_call | solution.py:379
  78.3 0.6 copy.7
Async XLA Ops:
  0.6 0.9 %copy-start = (f32[1024,32]{0,1:T(8,128)S(1)}, f32[1024,32]{0,1:T(8,128)}, u32[]{:S(2)}) copy-start(f32[1024,32]{0,1:T(8,128)} %param.4) | copy-start | bytes 393220
  1.5 0.7 copy-start.1

commit v3 on v2

--- a/solution.py
+++ b/solution.py
@@ -25,18 +25,27 @@
     for p in range(n):
         R=tiles[p]
         rows=[jnp.broadcast_to(R[k:k+1,:],(8,BLK)) for k in range(8)]
-        B={(k,i):jnp.broadcast_to(rows[k][:,8*p+i:8*p+i+1],(8,BLK)) for k in range(8) for i in range(k,8)}
+        C=[jnp.broadcast_to(R[:,8*p+i:8*p+i+1],(8,BLK)) for i in range(8)]
+        B={(k,i):jnp.broadcast_to(C[k][i:i+1,:],(8,BLK)) for k in range(8) for i in range(k,8)}
         inm=(lane>=8*p)&(lane<8*p+8)
         E=[jnp.where(inm,jnp.where(lane==8*p+k,1.0,0.0),rows[k]) for k in range(8)]
         m={}; rcp=[]; rs=[]
+        nxt=None
+        if p+1<n:
+            nc=[jnp.broadcast_to(tiles[p+1][:,8*p+k:8*p+k+1],(8,BLK)) for k in range(8)]
+            nxt=jnp.where(inm,0.0,tiles[p+1])
         for k in range(8):
-            r=lax.rsqrt(B[k,k]); rs.append(r); rc=r*r; rcp.append(rc)
+            rc=1.0/B[k,k]; rs.append(lax.rsqrt(B[k,k])); rcp.append(rc)
             for i in range(k+1,8):
                 m[i,k]=B[k,i]*rc
             for i in range(k+1,8):
                 for j in range(i,8):
                     B[i,j]=B[i,j]-m[i,k]*B[k,j]
                 E[i]=E[i]-m[i,k]*E[k]
+            if nxt is not None:
+                for i in range(k+1,8):
+                    nc[i]=nc[i]-m[i,k]*nc[k]
+                nxt=nxt-(nc[k]*rc)*E[k]
         V=[None]*8
         for k in reversed(range(8)):
             v=E[k]*rcp[k]
@@ -47,7 +56,8 @@
         for k in range(7):
             o=jnp.where(sub==k,E[k]*rs[k],o)
         out.append(jnp.where(lane<=8*p+sub,o,0.0))
-        for q in range(p+1,n):
+        if nxt is not None: tiles[p+1]=nxt
+        for q in range(p+2,n):
             c=[jnp.broadcast_to(tiles[q][:,8*p+k:8*p+k+1],(8,BLK)) for k in range(8)]
             t=jnp.where(inm,0.0,tiles[q])
             acc=[c[k]*V[k] for k in range(8)]
@@ -60,7 +70,7 @@
 MESH = pl.DeviceIdType.MESH
 
 
-def factor_blocks(a, u, x, s, arrive, hook):
+def factor_blocks(a, u, x, s, arrive, rest, hook):
     def step(b, _):
         for bb in range(4):
             o, e = bb * BLK, (bb + 1) * BLK
@@ -69,7 +79,7 @@
             def _():
                 arrive(bb)
                 if bb == 0:
-                    s[...] = a[0:BLK, :]
+                    s[:, 0:BLK] = a[0:BLK, 0:BLK]
                 else:
                     wt = u[0:o, o:e].T
                     s[:, :o] = -dot3(wt, x[0:o, 0:o], NN)
@@ -85,6 +95,9 @@
             @pl.when(b == bb)
             def _():
                 inv = x[o:e, o:e]
+                if bb == 0:
+                    rest()
+                    s[:, BLK:] = a[0:BLK, BLK:]
                 u[o:e, o:] = dot3(inv, s[:, o:], NN)
                 if bb > 0:
                     x[o:e, :o] = dot3(inv, s[:, :o], NN)
@@ -98,8 +111,8 @@
 
 
 def factor_kernel(
-    diag_ref, pt_ref, l_ref, x_ref, pr_ref, pc_ref, pack, strip, tb, a_ref, u_ref, s_ref,
-    s1, r1, s2, r2, sx, rx, sy, ry, sx2, rx2, sy2, ry2, st, s5, r5, s6, r6, own,
+    diag_in, pt_in, l_ref, x_ref, pr_ref, pc_ref, diag_ref, pt_ref, pack, strip, tb, a_ref, u_ref, s_ref,
+    s1, r1, s2, r2, s2b, r2b, sx, rx, sy, ry, sx2, rx2, sy2, ry2, st, s5, r5, s6, r6, own,
 ):
     r = lax.axis_index("row")
     c = lax.axis_index("col")
@@ -124,6 +137,12 @@
     def each(count, me, fn):
         loop(1, count, lambda t: fn(lax.rem(me + t, count)))
 
+    fetch = [
+        pltpu.make_async_copy(diag_in, diag_ref, own.at[0]),
+        pltpu.make_async_copy(pt_in, pt_ref, own.at[1]),
+    ]
+    for copy in fetch:
+        copy.start()
     barrier = pltpu.get_barrier_semaphore()
 
     def greet(row, col):
@@ -144,8 +163,12 @@
         return remote(part, part, s1.at[peer], r1.at[src], peer, c)
 
     def strip_copy(src, peer, q):
-        part = a_ref.at[at(src), q * BLK :]
+        part = a_ref.at[at(src), q * BLK :] if q else a_ref.at[at(src), 0:BLK]
         return remote(part, part, s2.at[peer], r2.at[src], r, peer)
+
+    def rest_copy(src, peer):
+        part = a_ref.at[at(src), BLK:]
+        return remote(part, part, s2b.at[peer], r2b.at[src], r, peer)
 
     def x_first(src, peer):
         return remote(pt_ref.at[:, left], pr_ref.at[at(4 * cy + src), left], sx.at[peer], rx.at[src], r, 4 * cy + peer)
@@ -194,9 +217,11 @@
     first = ((0, 2), (0, -2), (0, 1), (0, -1))
     relay = ((-2, 2), (-2, 1), (2, -1))
 
+    fetch[0].wait()
     block = diag_ref[...]
     pack[at8(r), :] = jnp.concatenate([block[pw * j : pw * j + pw, :] for j in range(w // pw)], axis=1)
     each(n, r, lambda p: diag_copy(r, p).start())
+    fetch[1].wait()
     keep = pltpu.make_async_copy(pt_ref, pr_ref.at[at(c), :], own.at[0])
     keep.start()
     each(4, cx, lambda p: x_first(cx, p).start())
@@ -219,14 +244,16 @@
     a_ref[at(c), :] = strip[...].T
     group = c // 4
 
-    def strips(fn):
+    def strips(fn, more):
         for q in range(4):
 
             @pl.when(group == q)
             def _():
                 each(n, c, lambda p: fn(p, q))
-
-    strips(lambda p, q: strip_copy(c, p, q).start())
+                if q == 0:
+                    each(n, c, more)
+
+    strips(lambda p, q: strip_copy(c, p, q).start(), lambda p: rest_copy(c, p).start())
 
     @pl.when(c != 0)
     def _():
@@ -269,6 +296,14 @@
             each(4, cy, lambda p: y_first(p, p).wait_recv())
             for j in range(4):
                 each(4, cx, lambda p: x_second(cx, p, j).start())
+
+    def rest():
+        def one(t):
+            @pl.when(t != c)
+            def _():
+                rest_copy(t, t).wait_recv()
+
+        loop(0, 4, one)
 
     def hook(bb):
         if bb == 0:
@@ -283,7 +318,7 @@
                 z_in(t).wait_recv()
                 twin_copy(t, core).start()
 
-    factor_blocks(a_ref, u_ref, x_ref, s_ref, arrive, hook)
+    factor_blocks(a_ref, u_ref, x_ref, s_ref, arrive, rest, hook)
 
     rows, cols = l_ref.shape
     per = BLK // w
@@ -294,7 +329,7 @@
     l_ref[...] = jnp.where(gi >= gj, turned, 0.0)
 
     each(n, r, lambda p: diag_copy(r, p).wait_send())
-    strips(lambda p, q: strip_copy(c, p, q).wait_send())
+    strips(lambda p, q: strip_copy(c, p, q).wait_send(), lambda p: rest_copy(c, p).wait_send())
     each(4, cx, lambda p: x_first(cx, p).wait_send())
     each(4, cy, lambda p: y_first(cy, p).wait_send())
     for i, (src, to) in enumerate(first + relay):
@@ -315,6 +350,7 @@
     dma = pltpu.SemaphoreType.DMA
     any_space = pl.BlockSpec(memory_space=pl.ANY)
     vmem = pl.BlockSpec(memory_space=pltpu.VMEM)
+    hbm = pl.BlockSpec(memory_space=pltpu.HBM)
     return pl.pallas_call(
         factor_kernel,
         out_shape=(
@@ -323,9 +359,11 @@
             jax.ShapeDtypeStruct((NB, m), F),
             jax.ShapeDtypeStruct((NB, m), F),
         ),
-        in_specs=[vmem, any_space],
+        in_specs=[hbm, hbm],
         out_specs=[vmem, vmem, any_space, any_space],
         scratch_shapes=[
+            pltpu.VMEM(diag.shape, F),
+            pltpu.VMEM((w, m), F),
             pltpu.VMEM((w * NB // BLK, BLK), F),
             pltpu.VMEM((NB, w), F),
             pltpu.VMEM((w, m), F),
@@ -333,8 +371,8 @@
             pltpu.VMEM((NB, NB), F),
             pltpu.VMEM((BLK, NB), F),
         ]
-        + [dma((16,))] * 4
-        + [dma((4,))] * 4
+        + [dma((16,))] * 5
+        + [dma((4,))] * 5
         + [dma((16,)), dma((16,)), dma((4,)), dma((4,))]
         + [dma((4,)), dma((8,)), dma((8,)), dma((8,)), dma((8,)), dma((2,))],
         compiler_params=pltpu.CompilerParams(
@@ -343,55 +381,79 @@
     )(diag, pt)
 
 
-def split_dot(ah, al, bh, bl, dims):
-    d = lambda x, y: lax.dot_general(x, y, (dims, ((), ())), preferred_element_type=F)
-    return d(ah, bh) + (d(ah, bl) + d(al, bh))
-
-
-def update_kernel(x_ref, pr_ref, pc_ref, slab_ref, out_ref, po_ref, xh, xl, ch, cl, tmp):
-    i = pl.program_id(0)
-
-    @pl.when(i == 0)
-    def _():
-        h, l = split(x_ref[...])
-        xh[...] = h
-        xl[...] = l
-        ph, plo = split(pc_ref[...])
-        f = split_dot(xh[...], xl[...], ph, plo, NN)
-        h, l = split(f)
-        ch[...] = h
-        cl[...] = l
-
-    ph, plo = split(pr_ref[...])
-    f = split_dot(xh[...], xl[...], ph, plo, NN)
-    tmp[...] = f
-    h, l = split(f.T)
-    out_ref[...] = slab_ref[...] - split_dot(h, l, ch[...], cl[...], NN)
+STEP = 256
+
+
+def update_kernel(l_in, x_ref, pr_ref, pc_ref, slab_ref, l_ref, po_ref, out_ref, xc, cc, buf, rows, sem_in, sem_out):
+    m, n = buf.shape
+    cut = lambda ref, j: ref.at[j * STEP : (j + 1) * STEP]
+    steps = range(m // STEP)
+    ins = [pltpu.make_async_copy(cut(slab_ref, j), cut(buf, j), sem_in.at[j]) for j in steps]
+    outs = [pltpu.make_async_copy(cut(buf, j), cut(out_ref, j), sem_out.at[j]) for j in steps]
     w = po_ref.shape[0]
-    po_ref[...] = tmp[pl.ds(pl.multiple_of(lax.axis_index("col") * w, w), w), :]
-
-
-def update(x, pr, pc, slab, w, tile=256):
+    mine = rows.at[pl.ds(pl.multiple_of(lax.axis_index("col") * w, w), w)]
+    outs.append(pltpu.make_async_copy(l_in, l_ref, sem_out.at[len(ins)]))
+    outs.append(pltpu.make_async_copy(mine, po_ref, sem_out.at[len(ins) + 1]))
+    for copy in ins:
+        copy.start()
+    outs[-2].start()
+
+    def dot(a, b):
+        return lax.dot_general(a, b, (NN, ((), ())), preferred_element_type=F)
+
+    h, l = split(x_ref[...])
+    xc[:, :NB] = h
+    xc[:, NB : 2 * NB] = l
+    xc[:, 2 * NB :] = h
+    h, l = split(pc_ref[...])
+    h, l = split(dot(xc[...], jnp.concatenate([h, h, l], axis=0)))
+    cc[:NB] = h
+    cc[NB : 2 * NB] = h
+    cc[2 * NB :] = l
+    h, l = split(pr_ref[...])
+    rows[...] = dot(xc[...], jnp.concatenate([h, h, l], axis=0))
+    outs[-1].start()
+    for j in steps:
+        h, l = split(rows[:, j * STEP : (j + 1) * STEP].T)
+        product = dot(jnp.concatenate([h, l, h], axis=1), cc[...])
+        ins[j].wait()
+        buf[j * STEP : (j + 1) * STEP] = buf[j * STEP : (j + 1) * STEP] - product
+        outs[j].start()
+    for copy in outs:
+        copy.wait()
+
+
+def update(factor, x, pr, pc, slab, w):
     m, n = slab.shape
-    full = lambda s: pl.BlockSpec(s, lambda i: (0, 0), pipeline_mode=pl.Buffered(1))
-    rows = lambda k: pl.BlockSpec((tile, k), lambda i: (i, 0))
-    cols = lambda k: pl.BlockSpec((k, tile), lambda i: (0, i))
+    vmem = pl.BlockSpec(memory_space=pltpu.VMEM)
+    any_space = pl.BlockSpec(memory_space=pl.ANY)
+    hbm = pl.BlockSpec(memory_space=pltpu.HBM)
+    dma = pltpu.SemaphoreType.DMA
     return pl.pallas_call(
         update_kernel,
-        grid=(m // tile,),
-        out_shape=(jax.ShapeDtypeStruct((m, n), F), jax.ShapeDtypeStruct((w, m), F)),
-        in_specs=[full((NB, NB)), cols(NB), full((NB, n)), rows(n)],
-        out_specs=[rows(n), cols(w)],
-        scratch_shapes=[pltpu.VMEM((NB, NB), jnp.bfloat16)] * 2
-        + [pltpu.VMEM((NB, n), jnp.bfloat16)] * 2
-        + [pltpu.VMEM((NB, tile), F)],
+        out_shape=(
+            jax.ShapeDtypeStruct(factor.shape, F),
+            jax.ShapeDtypeStruct((w, m), F),
+            jax.ShapeDtypeStruct((m, n), F),
+        ),
+        in_specs=[vmem, vmem, vmem, vmem, hbm],
+        out_specs=[hbm, hbm, hbm],
+        scratch_shapes=[
+            pltpu.VMEM((NB, 3 * NB), jnp.bfloat16),
+            pltpu.VMEM((3 * NB, n), jnp.bfloat16),
+            pltpu.VMEM((m, n), F),
+            pltpu.VMEM((NB, m), F),
+            dma((m // STEP,)),
+            dma((m // STEP + 2,)),
+        ],
         compiler_params=pltpu.CompilerParams(vmem_limit_bytes=48 << 20),
-    )(x, pr, pc, slab)
+    )(factor, x, pr, pc, slab)
 
 
 def body(diag_block, panel, slab):
-    factor_out, inverse, pr, pc = factor_and_gather(diag_block, panel.T)
-    out, panel_out = update(inverse, pr, pc, slab, panel.shape[1])
+    in_hbm = lambda v: pltpu.with_memory_space_constraint(v, pltpu.HBM)
+    factor, inverse, pr, pc = factor_and_gather(in_hbm(diag_block), in_hbm(panel.T))
+    factor_out, panel_out, out = update(factor, inverse, pr, pc, slab, panel.shape[1])
     return factor_out, panel_out.T, out
 
 

time: 79.1 us -> 66.2 us (0.84)
  the two profiles are of different devices: /device:TPU:33 before, /device:TPU:1 now
where the time goes in v3:
time: 66.2 us; the launch traced here: 65 us
  Pallas kernels  64.4 us (97%)
    pallas_call x1, Pallas kernels, factor_and_gather(): pl.pallas_call(factor_kernel, out_shape=(jax.ShapeDtypeStruct(diag.shape,...  55.6 us
    pallas_call x1, Pallas kernels, update(): pl.pallas_call(update_kernel, out_shape=(jax.ShapeDtypeStruct(factor.shap...  8.82 us

profile of v3, /device:TPU:1, one launch (start us, length us, event | category | flops | bytes accessed | tf_op | source)
XLA Modules:
  0.0 65.0 jit_solution(17836530147807022184)
XLA Ops:
  0.6 55.6 %shard_map.58 = (f32[32,32]{1,0:T(8,128)S(1)}, f32[512,512]{1,0:T(8,128)S(1)}, f32[512,1024]{1,0:T(8,128)S(1)}, f32[512,1024]{1,0:T(8,128)S(1)}) custom-call(f32[32,32]{1,0:T(8,128)} %diag_in.1, f32[32,1024]{1,0:T(8,128)} %bitcast.2), custom_call_target="tpu_custom_call" | custom-call | tf_op jit(solution)/shard_map/pallas_call | solution.py:354
  56.2 8.8 %shard_map.59 = (f32[32,32]{1,0:T(8,128)}, f32[32,1024]{1,0:T(8,128)}, f32[1024,1024]{1,0:T(8,128)}) custom-call(f32[32,32]{1,0:T(8,128)S(1)} %get-tuple-element.10.l_in, f32[512,512]{1,0:T(8,128)S(1)} %get-tuple-element.11.x_ref, f32[512,1024]{1,0:T(8,128)S(1)} %get-tuple-element.12.pr_ref, f32[512,1024]{1,0:T(8,128)S(1)} %get-tuple-element.13.pc_ref, ...), custom_call_target="tpu_custom_call" | custom-call | tf_op jit(solution)/shard_map/pallas_call | solution.py:432

commit v4 on v3

--- a/solution.py
+++ b/solution.py
@@ -17,12 +17,14 @@
     return d(ah,bh)+(d(ah,bl)+d(al,bh))
 NN=((1,),(0,)); NT=((1,),(1,))
 
-def sweep(tiles):
+def sweep(tiles, middle):
     lane=lax.broadcasted_iota(jnp.int32,(8,BLK),1)
     sub=lax.broadcasted_iota(jnp.int32,(8,BLK),0)
     n=len(tiles); out=[]
     tiles=list(tiles)
     for p in range(n):
+        if p == n // 2:
+            middle()
         R=tiles[p]
         rows=[jnp.broadcast_to(R[k:k+1,:],(8,BLK)) for k in range(8)]
         C=[jnp.broadcast_to(R[:,8*p+i:8*p+i+1],(8,BLK)) for i in range(8)]
@@ -70,7 +72,7 @@
 MESH = pl.DeviceIdType.MESH
 
 
-def factor_blocks(a, u, x, s, arrive, rest, hook):
+def factor_blocks(a, u, x, s, arrive, middle, rest, hook):
     def step(b, _):
         for bb in range(4):
             o, e = bb * BLK, (bb + 1) * BLK
@@ -86,7 +88,7 @@
                     s[:, o:] = a[o:e, o:] - dot3(wt, u[0:o, o:], NN)
 
         off = pl.multiple_of(b * BLK, BLK)
-        out = sweep([s[8 * t : 8 * t + 8, pl.ds(off, BLK)] for t in range(16)])
+        out = sweep([s[8 * t : 8 * t + 8, pl.ds(off, BLK)] for t in range(16)], lambda: middle(b))
         for t in range(16):
             x[pl.ds(pl.multiple_of(off + 8 * t, 8), 8), pl.ds(off, BLK)] = out[t]
         for bb in range(4):
@@ -224,8 +226,6 @@
     fetch[1].wait()
     keep = pltpu.make_async_copy(pt_ref, pr_ref.at[at(c), :], own.at[0])
     keep.start()
-    each(4, cx, lambda p: x_first(cx, p).start())
-    each(4, cy, lambda p: y_first(cy, p).start())
 
     @pl.when(c != 0)
     def _():
@@ -244,16 +244,14 @@
     a_ref[at(c), :] = strip[...].T
     group = c // 4
 
-    def strips(fn, more):
-        for q in range(4):
+    def strips(fn, groups):
+        for q in groups:
 
             @pl.when(group == q)
             def _():
                 each(n, c, lambda p: fn(p, q))
-                if q == 0:
-                    each(n, c, more)
-
-    strips(lambda p, q: strip_copy(c, p, q).start(), lambda p: rest_copy(c, p).start())
+
+    strips(lambda p, q: strip_copy(c, p, q).start(), (0,))
 
     @pl.when(c != 0)
     def _():
@@ -270,6 +268,9 @@
     @pl.when(away == c)
     def _():
         turn_local(tb, pc_ref.at[at(c), :]).start()
+
+    strips(lambda p, q: rest_copy(c, p).start(), (0,))
+    strips(lambda p, q: strip_copy(c, p, q).start(), (1, 2, 3))
 
     def arrive(bb):
         def one(t):
@@ -279,7 +280,12 @@
 
         loop(4 * bb, 4 * bb + 4, one)
         if bb == 0:
-
+            each(4, cx, lambda p: x_first(cx, p).start())
+            each(4, cy, lambda p: y_first(cy, p).start())
+
+    def middle(b):
+        @pl.when(b == 0)
+        def _():
             @pl.when(away != c)
             def _():
                 turn_plane_in().wait()
@@ -290,6 +296,39 @@
 
             for i, (src, to) in enumerate(first):
                 z_copy(i, src, to).start()
+            twin_copy(0, core).start()
+
+        @pl.when(b == 1)
+        def _():
+            z_in(-2).wait_recv()
+            z_in(2).wait_recv()
+            for i, (src, to) in enumerate(relay):
+                z_copy(4 + i, src, to).start()
+            for t in (2, -2):
+                twin_copy(t, core).start()
+
+        @pl.when(b == 2)
+        def _():
+            for t in (1, -1):
+                z_in(t).wait_recv()
+                twin_copy(t, core).start()
+
+        @pl.when(b == 3)
+        def _():
+            for t in (4, 3, -3):
+                z_in(t).wait_recv()
+                twin_copy(t, core).start()
+
+    def rest():
+        def one(t):
+            @pl.when(t != c)
+            def _():
+                rest_copy(t, t).wait_recv()
+
+        loop(0, 4, one)
+
+    def hook(bb):
+        if bb == 0:
             keep.wait()
             each(4, cx, lambda p: x_first(p, p).wait_recv())
             each(4, cy, lambda p: y_second(cy, p).start())
@@ -297,28 +336,7 @@
             for j in range(4):
                 each(4, cx, lambda p: x_second(cx, p, j).start())
 
-    def rest():
-        def one(t):
-            @pl.when(t != c)
-            def _():
-                rest_copy(t, t).wait_recv()
-
-        loop(0, 4, one)
-
-    def hook(bb):
-        if bb == 0:
-            z_in(-2).wait_recv()
-            z_in(2).wait_recv()
-            for i, (src, to) in enumerate(relay):
-                z_copy(4 + i, src, to).start()
-            for t in (0, 2, -2):
-                twin_copy(t, core).start()
-        if bb == 2:
-            for t in (1, -1, 3, -3, 4):
-                z_in(t).wait_recv()
-                twin_copy(t, core).start()
-
-    factor_blocks(a_ref, u_ref, x_ref, s_ref, arrive, rest, hook)
+    factor_blocks(a_ref, u_ref, x_ref, s_ref, arrive, middle, rest, hook)
 
     rows, cols = l_ref.shape
     per = BLK // w
@@ -329,7 +347,8 @@
     l_ref[...] = jnp.where(gi >= gj, turned, 0.0)
 
     each(n, r, lambda p: diag_copy(r, p).wait_send())
-    strips(lambda p, q: strip_copy(c, p, q).wait_send(), lambda p: rest_copy(c, p).wait_send())
+    strips(lambda p, q: rest_copy(c, p).wait_send(), (0,))
+    strips(lambda p, q: strip_copy(c, p, q).wait_send(), (0, 1, 2, 3))
     each(4, cx, lambda p: x_first(cx, p).wait_send())
     each(4, cy, lambda p: y_first(cy, p).wait_send())
     for i, (src, to) in enumerate(first + relay):

time: 66.2 us -> 62.2 us (0.940); the launches traced: 65 us -> 62 us
  Pallas kernels: 64.4 us -> 61.3 us
    pallas_call x1, Pallas kernels: 55.6 us -> 52.5 us  [factor_and_gather(): pl.pallas_call(factor_kernel, out_shape=(jax.ShapeDtypeStruct(diag.shape,...]
where the time goes in v4:
time: 62.2 us; the launch traced here: 62 us
  Pallas kernels  61.3 us (99%)
  between operations  0.64 us (1%)
    pallas_call x1, Pallas kernels, factor_and_gather(): pl.pallas_call(factor_kernel, out_shape=(jax.ShapeDtypeStruct(diag.shape,...  52.5 us
    pallas_call x1, Pallas kernels, update(): pl.pallas_call(update_kernel, out_shape=(jax.ShapeDtypeStruct(factor.shap...  8.82 us

profile of v4, /device:TPU:1, one launch (start us, length us, event | category | flops | bytes accessed | tf_op | source)
XLA Modules:
  0.0 62.0 jit_solution(16993884849130516320)
XLA Ops:
  0.6 52.5 %shard_map.58 = (f32[32,32]{1,0:T(8,128)S(1)}, f32[512,512]{1,0:T(8,128)S(1)}, f32[512,1024]{1,0:T(8,128)S(1)}, f32[512,1024]{1,0:T(8,128)S(1)}) custom-call(f32[32,32]{1,0:T(8,128)} %diag_in.1, f32[32,1024]{1,0:T(8,128)} %bitcast.2), custom_call_target="tpu_custom_call" | custom-call | tf_op jit(solution)/shard_map/pallas_call | solution.py:373
  53.2 8.8 %shard_map.59 = (f32[32,32]{1,0:T(8,128)}, f32[32,1024]{1,0:T(8,128)}, f32[1024,1024]{1,0:T(8,128)}) custom-call(f32[32,32]{1,0:T(8,128)S(1)} %get-tuple-element.10.l_in, f32[512,512]{1,0:T(8,128)S(1)} %get-tuple-element.11.x_ref, f32[512,1024]{1,0:T(8,128)S(1)} %get-tuple-element.12.pr_ref, f32[512,1024]{1,0:T(8,128)S(1)} %get-tuple-element.13.pc_ref, ...), custom_call_target="tpu_custom_call" | custom-call | tf_op jit(solution)/shard_map/pallas_call | solution.py:451

commit v5 on v4

--- a/solution.py
+++ b/solution.py
@@ -157,34 +157,41 @@
     def remote(src, dst, send, recv, row, col):
         return pltpu.make_async_remote_copy(src, dst, send, recv, device_id=(row, col), device_id_type=MESH)
 
+    def wait_all(part, send, recv, sent):
+        every = remote(part, part, send, recv, r, c)
+        if sent:
+            every.wait_send()
+        else:
+            every.wait_recv()
+
     pw = pack.shape[0] // n
     at8 = lambda i: pl.ds(pl.multiple_of(i * pw, pw), pw)
 
     def diag_copy(src, peer):
         part = pack.at[at8(src), :]
-        return remote(part, part, s1.at[peer], r1.at[src], peer, c)
+        return remote(part, part, s1, r1, peer, c)
 
     def strip_copy(src, peer, q):
         part = a_ref.at[at(src), q * BLK :] if q else a_ref.at[at(src), 0:BLK]
-        return remote(part, part, s2.at[peer], r2.at[src], r, peer)
+        return remote(part, part, s2, r2.at[src], r, peer)
 
     def rest_copy(src, peer):
         part = a_ref.at[at(src), BLK:]
-        return remote(part, part, s2b.at[peer], r2b.at[src], r, peer)
+        return remote(part, part, s2b, r2b.at[src], r, peer)
 
     def x_first(src, peer):
-        return remote(pt_ref.at[:, left], pr_ref.at[at(4 * cy + src), left], sx.at[peer], rx.at[src], r, 4 * cy + peer)
+        return remote(pt_ref.at[:, left], pr_ref.at[at(4 * cy + src), left], sx, rx, r, 4 * cy + peer)
 
     def y_first(src, peer):
-        return remote(pt_ref.at[:, right], pr_ref.at[at(4 * src + cx), right], sy.at[peer], ry.at[src], r, 4 * peer + cx)
+        return remote(pt_ref.at[:, right], pr_ref.at[at(4 * src + cx), right], sy, ry, r, 4 * peer + cx)
 
     def y_second(src, peer):
         part = pr_ref.at[at4(src), left]
-        return remote(part, part, sy2.at[peer], ry2.at[src], r, 4 * peer + cx)
+        return remote(part, part, sy2, ry2, r, 4 * peer + cx)
 
     def x_second(src, peer, j):
         part = pr_ref.at[at(4 * j + src), right]
-        return remote(part, part, sx2.at[4 * peer + j], rx2.at[4 * src + j], r, 4 * cy + peer)
+        return remote(part, part, sx2, rx2, r, 4 * cy + peer)
 
     def turn_z():
         return remote(pt_ref, tb, st.at[0], st.at[1], lax.rem(r + c, n), c)
@@ -206,15 +213,15 @@
 
     def z_copy(i, src, to):
         part = piece(src, core)
-        return remote(part, part, s5.at[i], r5.at[(src - to) % 8], z_row(to), c)
+        return remote(part, part, s5, r5.at[(src - to) % 8], z_row(to), c)
 
     def z_in(src):
         part = piece(src, core)
-        return remote(part, part, s5.at[0], r5.at[src % 8], r, c)
+        return remote(part, part, s5, r5.at[src % 8], r, c)
 
     def twin_copy(t, side):
         part = piece(t, side)
-        return remote(part, part, s6.at[t % 8], r6.at[t % 8], other, c)
+        return remote(part, part, s6, r6, other, c)
 
     first = ((0, 2), (0, -2), (0, 1), (0, -1))
     relay = ((-2, 2), (-2, 1), (2, -1))
@@ -235,7 +242,7 @@
     def _():
         turn_local(pt_ref, tb).start()
 
-    each(n, r, lambda p: diag_copy(p, p).wait_recv())
+    wait_all(pack.at[0 : (n - 1) * pw], s1, r1, False)
     for i in range(n):
         packed = pack[pw * i : pw * i + pw, :]
         for j in range(w // pw):
@@ -330,9 +337,9 @@
     def hook(bb):
         if bb == 0:
             keep.wait()
-            each(4, cx, lambda p: x_first(p, p).wait_recv())
+            wait_all(pr_ref.at[0 : 3 * w, left], sx, rx, False)
             each(4, cy, lambda p: y_second(cy, p).start())
-            each(4, cy, lambda p: y_first(p, p).wait_recv())
+            wait_all(pr_ref.at[0 : 3 * w, right], sy, ry, False)
             for j in range(4):
                 each(4, cx, lambda p: x_second(cx, p, j).start())
 
@@ -346,22 +353,24 @@
     gj = c * w + lax.broadcasted_iota(jnp.int32, (rows, cols), 1)
     l_ref[...] = jnp.where(gi >= gj, turned, 0.0)
 
-    each(n, r, lambda p: diag_copy(r, p).wait_send())
-    strips(lambda p, q: rest_copy(c, p).wait_send(), (0,))
-    strips(lambda p, q: strip_copy(c, p, q).wait_send(), (0, 1, 2, 3))
-    each(4, cx, lambda p: x_first(cx, p).wait_send())
-    each(4, cy, lambda p: y_first(cy, p).wait_send())
-    for i, (src, to) in enumerate(first + relay):
-        z_copy(i, src, to).wait_send()
-    each(4, cy, lambda p: y_second(cy, p).wait_send())
-    each(4, cy, lambda p: y_second(p, p).wait_recv())
-    for j in range(4):
-        each(4, cx, lambda p: x_second(cx, p, j).wait_send())
-        each(4, cx, lambda p: x_second(p, p, j).wait_recv())
-
-    for t in range(8):
-        twin_copy(t, core).wait_send()
-        twin_copy(t, 1 - core).wait_recv()
+    wait_all(pack.at[0 : (n - 1) * pw], s1, r1, True)
+    for q in range(4):
+
+        @pl.when(group == q)
+        def _():
+            if q == 0:
+                wait_all(a_ref.at[0 : (n - 1) * w, 0:BLK], s2, r2.at[0], True)
+                wait_all(a_ref.at[0 : (n - 1) * w, BLK:], s2b, r2b.at[0], True)
+            else:
+                wait_all(a_ref.at[0 : (n - 1) * w, q * BLK :], s2, r2.at[0], True)
+
+    wait_all(pr_ref.at[0 : 3 * w, left], sx, rx, True)
+    wait_all(pr_ref.at[0 : 3 * w, right], sy, ry, True)
+    wait_all(pc_ref.at[0 : 7 * w, :], s5, r5.at[0], True)
+    for sent in (True, False):
+        wait_all(pr_ref.at[0 : 12 * w, left], sy2, ry2, sent)
+        wait_all(pr_ref.at[0 : 12 * w, right], sx2, rx2, sent)
+        wait_all(pc_ref.at[0 : 8 * w, :], s6, r6, sent)
 
 
 def factor_and_gather(diag, pt):
@@ -390,10 +399,7 @@
             pltpu.VMEM((NB, NB), F),
             pltpu.VMEM((BLK, NB), F),
         ]
-        + [dma((16,))] * 5
-        + [dma((4,))] * 5
-        + [dma((16,)), dma((16,)), dma((4,)), dma((4,))]
-        + [dma((4,)), dma((8,)), dma((8,)), dma((8,)), dma((8,)), dma((2,))],
+        + [dma(()), dma(()), dma(()), dma((16,)), dma(()), dma((4,)), dma(()), dma(()), dma(()), dma(()), dma(()), dma(()), dma(()), dma(()), dma((4,)), dma(()), dma((8,)), dma(()), dma(()), dma((2,))],
         compiler_params=pltpu.CompilerParams(
             vmem_limit_bytes=40 << 20, collective_id=0, has_side_effects=True
         ),

time: 62.2 us -> 60.5 us (0.973)
  Pallas kernels: 61.3 us -> 59.2 us
    pallas_call x1, Pallas kernels: 52.5 us -> 50.4 us  [factor_and_gather(): pl.pallas_call(factor_kernel, out_shape=(jax.ShapeDtypeStruct(diag.shape,...]
where the time goes in v5:
time: 60.5 us; the launch traced here: 59.8 us
  Pallas kernels  59.2 us (98%)
  between operations  0.64 us (1%)
    pallas_call x1, Pallas kernels, factor_and_gather(): pl.pallas_call(factor_kernel, out_shape=(jax.ShapeDtypeStruct(diag.shape,...  50.4 us
    pallas_call x1, Pallas kernels, update(): pl.pallas_call(update_kernel, out_shape=(jax.ShapeDtypeStruct(factor.shap...  8.82 us

profile of v5, /device:TPU:1, one launch (start us, length us, event | category | flops | bytes accessed | tf_op | source)
XLA Modules:
  0.0 59.8 jit_solution(10060364656545914821)
XLA Ops:
  0.6 50.4 %shard_map.58 = (f32[32,32]{1,0:T(8,128)S(1)}, f32[512,512]{1,0:T(8,128)S(1)}, f32[512,1024]{1,0:T(8,128)S(1)}, f32[512,1024]{1,0:T(8,128)S(1)}) custom-call(f32[32,32]{1,0:T(8,128)} %diag_in.1, f32[32,1024]{1,0:T(8,128)} %bitcast.2), custom_call_target="tpu_custom_call" | custom-call | tf_op jit(solution)/shard_map/pallas_call | solution.py:382
  51.0 8.8 %shard_map.59 = (f32[32,32]{1,0:T(8,128)}, f32[32,1024]{1,0:T(8,128)}, f32[1024,1024]{1,0:T(8,128)}) custom-call(f32[32,32]{1,0:T(8,128)S(1)} %get-tuple-element.10.l_in, f32[512,512]{1,0:T(8,128)S(1)} %get-tuple-element.11.x_ref, f32[512,1024]{1,0:T(8,128)S(1)} %get-tuple-element.12.pr_ref, f32[512,1024]{1,0:T(8,128)S(1)} %get-tuple-element.13.pc_ref, ...), custom_call_target="tpu_custom_call" | custom-call | tf_op jit(solution)/shard_map/pallas_call | solution.py:457

commit v6 on v5

--- a/solution.py
+++ b/solution.py
@@ -23,7 +23,7 @@
     n=len(tiles); out=[]
     tiles=list(tiles)
     for p in range(n):
-        if p == n // 2:
+        if p == 5 * n // 8:
             middle()
         R=tiles[p]
         rows=[jnp.broadcast_to(R[k:k+1,:],(8,BLK)) for k in range(8)]
@@ -307,12 +307,12 @@
 
         @pl.when(b == 1)
         def _():
-            z_in(-2).wait_recv()
-            z_in(2).wait_recv()
-            for i, (src, to) in enumerate(relay):
-                z_copy(4 + i, src, to).start()
-            for t in (2, -2):
-                twin_copy(t, core).start()
+            for ready in (-2, 2):
+                z_in(ready).wait_recv()
+                for i, (src, to) in enumerate(relay):
+                    if src == ready:
+                        z_copy(4 + i, src, to).start()
+                twin_copy(ready, core).start()
 
         @pl.when(b == 2)
         def _():

time: 60.5 us -> 60.5 us (level)
  no operation moved by 1% of the time
where the time goes in v6:
time: 60.5 us; the launch traced here: 59.7 us
  Pallas kernels  59.1 us (98%)
  between operations  0.64 us (1%)
    pallas_call x1, Pallas kernels, factor_and_gather(): pl.pallas_call(factor_kernel, out_shape=(jax.ShapeDtypeStruct(diag.shape,...  50.2 us
    pallas_call x1, Pallas kernels, update(): pl.pallas_call(update_kernel, out_shape=(jax.ShapeDtypeStruct(factor.shap...  8.83 us

profile of v6, /device:TPU:1, one launch (start us, length us, event | category | flops | bytes accessed | tf_op | source)
XLA Modules:
  0.0 59.7 jit_solution(3860842086808292396)
XLA Ops:
  0.6 50.2 %shard_map.58 = (f32[32,32]{1,0:T(8,128)S(1)}, f32[512,512]{1,0:T(8,128)S(1)}, f32[512,1024]{1,0:T(8,128)S(1)}, f32[512,1024]{1,0:T(8,128)S(1)}) custom-call(f32[32,32]{1,0:T(8,128)} %diag_in.1, f32[32,1024]{1,0:T(8,128)} %bitcast.2), custom_call_target="tpu_custom_call" | custom-call | tf_op jit(solution)/shard_map/pallas_call | solution.py:382
  50.9 8.8 %shard_map.59 = (f32[32,32]{1,0:T(8,128)}, f32[32,1024]{1,0:T(8,128)}, f32[1024,1024]{1,0:T(8,128)}) custom-call(f32[32,32]{1,0:T(8,128)S(1)} %get-tuple-element.10.l_in, f32[512,512]{1,0:T(8,128)S(1)} %get-tuple-element.11.x_ref, f32[512,1024]{1,0:T(8,128)S(1)} %get-tuple-element.12.pr_ref, f32[512,1024]{1,0:T(8,128)S(1)} %get-tuple-element.13.pc_ref, ...), custom_call_target="tpu_custom_call" | custom-call | tf_op jit(solution)/shard_map/pallas_call | solution.py:457
